TPU v7x, 256 devices: a whole 4x4x8 slice. The times are simulated.
256 devices in a mesh: tower: 16 (over z_lo, y, core), dev: 16 (over z_hi, x).
Axes of the slice: x: 4, y: 4, z: 8 (z_hi: 4, z_lo: 2; z = z_hi * 2 + z_lo), core: 2. Of those that a mesh axis runs over, the one named last changes fastest.
Arguments:
- bag_ids: int32 [16, 8192, 32, 4], P('tower', None, 'dev'), may hold values from 0 to 1023
- bag_lengths: int32 [16, 8192, 32], P('tower', None, 'dev'), may hold values from 1 to 4
- tables: bfloat16 [16, 32, 1024, 128], P('tower', 'dev'), may hold values from -3 to 3
- cross_down: bfloat16 [16, 1, 4096, 512], P('tower'), may hold values from -0.09375 to 0.09375
- cross_up: bfloat16 [16, 1, 512, 4096], P('tower'), may hold values from -0.25 to 0.25
- cross_bias: float32 [16, 1, 4096], P('tower'), may hold values from -4 to 4
- proj_weight: bfloat16 [16, 4096, 512], P('tower'), may hold values from -0.09375 to 0.09375
- proj_bias: float32 [16, 512], P('tower'), may hold values from -3 to 3
Outputs:
- interactions: float32 [8192, 120], P(('tower', 'dev'))
Inputs may be any that keep to these rules, and one draw needn't show every extreme that they name: `bag_ids`: where table rows travel between devices, each is sent as a whole 32-bit integer, one to a slot; a program may not pack several table rows into one word. `bag_lengths`: where bag lengths travel between devices, a program may pack several of them into one word.
All inputs are finite; a program needn't handle non-finite values.
Results may differ from a plain program's by a relative error of at most 0.0071.
Values may be sent and summed in bfloat16 or wider, within the bound.
A program may use at most 128 MiB of HBM per device.

v0:
```python
import jax
import jax.numpy as jnp
import numpy as np
from jax import lax
from jax.sharding import PartitionSpec as P

EMB = 128
OUT = 512


def pool_rows(tables_one, ids_one, lengths_one):
    table_rows = tables_one.shape[1]
    positions = lax.iota(jnp.int32, table_rows)
    counts = jnp.zeros(ids_one.shape[:2] + (table_rows,), jnp.bfloat16)
    for slot_index in range(ids_one.shape[2]):
        matched = (ids_one[:, :, slot_index, None] == positions) & (slot_index < lengths_one)[
            :, :, None
        ]
        counts = counts + matched.astype(jnp.bfloat16)
    summed = jnp.einsum("sft,ftd->sfd", counts, tables_one, preferred_element_type=jnp.float32)
    return summed.astype(jnp.bfloat16)


def tower_forward(base, down, up, bias, proj, proj_b):
    base_f = base.astype(jnp.float32)
    cross = base
    low = jnp.dot(cross, down[0], preferred_element_type=jnp.float32).astype(jnp.bfloat16)
    high = jnp.dot(low, up[0], preferred_element_type=jnp.float32) + bias[0]
    cross = (base_f * high + cross.astype(jnp.float32)).astype(jnp.bfloat16)
    return (jnp.dot(cross, proj, preferred_element_type=jnp.float32) + proj_b).astype(jnp.bfloat16)


def local(bag_ids, bag_lengths, tables, cross_down, cross_up, cross_bias, proj_weight, proj_bias):
    towers = lax.axis_size("tower")
    members = lax.axis_size("dev")
    samples = bag_ids.shape[1]
    block = samples // (towers * members)
    feat_dev = bag_ids.shape[2]
    slots = bag_ids.shape[3]
    weights = (cross_down[0], cross_up[0], cross_bias[0], proj_weight[0], proj_bias[0])
    every_table = lax.all_gather(tables[0], "dev", axis=0, tiled=True)
    keyed = bag_ids[0].reshape(towers, members, block, feat_dev, slots)
    counted = bag_lengths[0].reshape(towers, members, block, feat_dev)
    index = lax.all_to_all(keyed, "dev", split_axis=1, concat_axis=3, tiled=True)
    lengths_here = lax.all_to_all(counted, "dev", split_axis=1, concat_axis=3, tiled=True)
    count = index.shape[2]
    pooled = pool_rows(
        every_table,
        index.reshape(towers * count, -1, slots),
        lengths_here.reshape(towers * count, -1),
    )
    pooled_block = pooled.reshape(towers, 1, count, -1, EMB)
    finish_count = pooled_block.shape[2]
    rows = pooled_block.reshape(towers * finish_count, -1)
    outputs = tower_forward(rows, *weights).reshape(towers, finish_count, -1)
    gathered = lax.all_to_all(outputs, "tower", split_axis=0, concat_axis=0, tiled=True)
    gram = jnp.einsum(
        "isk,jsk->sij", gathered, gathered, preferred_element_type=jnp.float32
    ) / jnp.sqrt(jnp.float32(OUT))
    upper, lower = np.triu_indices(towers, 1)
    return gram[:, upper, lower]


def solution(mesh):
    placed = (
        P("tower", None, "dev", None),
        P("tower", None, "dev"),
        P("tower", "dev", None, None),
        P("tower", None, None, None),
        P("tower", None, None, None),
        P("tower", None, None),
        P("tower", None, None),
        P("tower", None),
    )
    return jax.shard_map(
        local, mesh=mesh, in_specs=placed, out_specs=P(("tower", "dev"), None), check_vma=False
    )
```

profile of v0, /device:TPU:1, one launch (start us, length us, event | category | flops | bytes accessed | tf_op | source)
XLA Modules:
  0.0 205.6 jit_solution(1138326824918847656)
XLA Ops:
  6.5 0.7 all-gather.3.cloned.1.call-update
  7.3 1.0 reshape_squeeze.7
  8.4 0.8 reshape.57
  9.1 11.6 %all-to-all-start.1 = ((s32[16,1,1024]{2,1,0:T(1,128)}), s32[16,1,1024]{2,1,0:T(1,128)S(1)}, u32[]{:S(2)}, u32[]{:S(2)}) async-start(s32[16,1,1024]{2,1,0:T(1,128)} %reshape.57), calls=%async_computation.1 | async-start | bytes 131072 | tf_op jit(solution)/shard_map/all_to_all | solution.py:45
  20.7 1.3 reshape_squeeze.6
  22.0 0.3 copy.46
  22.4 1.2 reshape.55
  23.5 6.1 %all-to-all-done.1 = s32[16,1,1024]{2,1,0:T(1,128)S(1)} async-done(((s32[16,1,1024]{2,1,0:T(1,128)}), s32[16,1,1024]{2,1,0:T(1,128)S(1)}, u32[]{:S(2)}, u32[]{:S(2)}) %all-to-all-start.1) | async-done | bytes 65568 | tf_op jit(solution)/shard_map/all_to_all | solution.py:45
  29.7 3.5 %all-to-all-start = ((s32[16,1,4096]{2,1,0:T(1,128)}), s32[16,1,4096]{2,1,0:T(1,128)S(1)}, u32[]{:S(2)}, u32[]{:S(2)}) async-start(s32[16,1,4096]{2,1,0:T(1,128)} %reshape.55), calls=%async_computation | async-start | bytes 524288 | tf_op jit(solution)/shard_map/all_to_all | solution.py:44
  33.2 0.5 broadcast.60
  33.7 0.8 reduce.1
  34.5 0.1 reshape.58
  34.6 0.1 compare_bitcast_fusion.3
  34.8 0.2 gt.80
  34.9 0.2 gt.95
  35.1 0.2 gt.90
  35.2 0.2 gt.85
  35.4 17.6 %all-to-all-done = s32[16,1,4096]{2,1,0:T(1,128)S(1)} async-done(((s32[16,1,4096]{2,1,0:T(1,128)}), s32[16,1,4096]{2,1,0:T(1,128)S(1)}, u32[]{:S(2)}, u32[]{:S(2)}) %all-to-all-start) | async-done | bytes 262176 | tf_op jit(solution)/shard_map/all_to_all | solution.py:44
  53.0 1.3 reduce
  54.2 0.3 reshape.56
  54.8 0.4 reshape.46
  55.2 57.7 %fusion.53 = bf16[512,32,1024]{2,0,1:T(8,128)(2,1)} fusion(s32[512,32]{0,1:T(8,128)S(1)} %get-tuple-element.10, s32[512,32]{0,1:T(8,128)S(1)} %get-tuple-element.11, s32[512,32]{0,1:T(8,128)S(1)} %get-tuple-element.12, s32[512,32]{0,1:T(8,128)S(1)} %get-tuple-element.9, pred[512,32]{0,1:T(8,128)(4,1)S(1)} %gt.95, ...), kind=kLoop, calls=%fused_computation.13.clone.clone.clone.clone.1 | loop fusion | flops 335544320 | bytes 33882112 | tf_op jit(solution)/shard_map/sft,ftd->sfd/dot_general | solution.py:20
  113.0 14.5 %all-gather.3.cloned.1.call-done = bf16[1,32,1024,128]{3,2,0,1:T(8,128)(2,1)} async-done(((bf16[1,2,1024,128]{3,2,0,1:T(8,128)(2,1)}), bf16[1,32,1024,128]{3,2,0,1:T(8,128)(2,1)}) %all-gather.3.cloned.1.call-update) | async-done | bytes 8388624 | tf_op jit(solution)/shard_map/all_gather | solution.py:41
  127.5 18.9 %fusion.31 = bf16[32,512,128]{1,2,0:T(8,128)(2,1)} fusion(bf16[1,32,1024,128]{3,2,0,1:T(8,128)(2,1)} %all-gather.3.cloned.1.call-done, bf16[512,32,1024]{2,0,1:T(8,128)(2,1)} %fusion.53), kind=kOutput, calls=%fused_computation.33 | convolution fusion | flops 4297064448 | bytes 46137344 | tf_op jit(solution)/shard_map/sft,ftd->sfd/dot_general | solution.py:20
  146.3 6.4 %copy.37 = bf16[512,4096]{1,0:T(8,128)(2,1)} copy(bf16[512,4096]{0,1:T(8,128)(2,1)} %bitcast.98) | data formatting | bytes 8388608 | tf_op jit(solution)/shard_map/reshape;reshape | solution.py:54
  152.8 12.7 %fusion.24 = bf16[512,4096]{1,0:T(8,128)(2,1)} fusion(bf16[512,4096]{1,0:T(8,128)(2,1)} %copy.37, bf16[1,1,512,4096]{3,2,1,0:T(8,128)(2,1)} %param.16, f32[4096]{0:T(1024)S(1)} %bitcast.104, bf16[512,4096]{0,1:T(8,128)(2,1)} %bitcast.99, bf16[1,1,4096,512]{3,2,1,0:T(8,128)(2,1)} %param.15), kind=kOutput, calls=%fused_computation.26 | convolution fusion | flops 4305715200 | bytes 20987904 | tf_op jit(solution)/shard_map/dot_general | solution.py:28
  165.5 5.8 %fusion.39 = bf16[512,512]{1,0:T(8,128)(2,1)S(1)} fusion(bf16[512,4096]{1,0:T(8,128)(2,1)} %fusion.24, bf16[1,4096,512]{2,1,0:T(8,128)(2,1)} %param.18, f32[512]{0:T(512)S(1)} %bitcast.105), kind=kOutput, calls=%fused_computation.35 | convolution fusion | flops 2148007936 | bytes 8914944 | tf_op jit(solution)/shard_map/dot_general | solution.py:30
  171.3 24.6 %all_to_all.29 = bf16[16,32,512]{2,1,0:T(8,128)(2,1)S(1)} all-to-all(bf16[16,32,512]{2,1,0:T(8,128)(2,1)S(1)} %bitcast.102), channel_id=1, replica_groups=mesh['tower'=16,'dev'=16] {'tower'}, dimensions={0} | all-to-all | bytes 1048576 | tf_op jit(solution)/shard_map/all_to_all | solution.py:56
  195.9 0.4 convolution_multiply_fusion
  196.3 0.2 copy.40
  196.5 1.6 gather_fusion
  198.1 0.7 copy.41
  (11 shorter events, 0.3 us)
Async XLA Ops:
  6.5 120.9 %all-gather.3.cloned.1.call-start = ((), (), s32[]{:S(2)}) async-start(), calls=%async_computation.3 | async-start | bytes 8912896 | tf_op jit(solution)/shard_map/all_gather | solution.py:41
  9.1 20.5 %all-to-all-start.1 = ((s32[16,1,1024]{2,1,0:T(1,128)}), s32[16,1,1024]{2,1,0:T(1,128)S(1)}, u32[]{:S(2)}, u32[]{:S(2)}) async-start(s32[16,1,1024]{2,1,0:T(1,128)} %reshape.57), calls=%async_computation.1 | async-start | bytes 131072 | tf_op jit(solution)/shard_map/all_to_all | solution.py:45
  29.7 23.3 %all-to-all-start = ((s32[16,1,4096]{2,1,0:T(1,128)}), s32[16,1,4096]{2,1,0:T(1,128)S(1)}, u32[]{:S(2)}, u32[]{:S(2)}) async-start(s32[16,1,4096]{2,1,0:T(1,128)} %reshape.55), calls=%async_computation | async-start | bytes 524288 | tf_op jit(solution)/shard_map/all_to_all | solution.py:44
  146.3 6.5 %copy-start.1 = (f32[1,1,4096]{2,1,0:T(1,128)S(1)}, f32[1,1,4096]{2,1,0:T(1,128)}, u32[]{:S(2)}) copy-start(f32[1,1,4096]{2,1,0:T(1,128)} %param.17) | copy-start | bytes 49156
  152.8 12.7 %copy-start.2 = (f32[1,512]{1,0:T(1,128)S(1)}, f32[1,512]{1,0:T(1,128)}, u32[]{:S(2)}) copy-start(f32[1,512]{1,0:T(1,128)} %param.19) | copy-start | bytes 6148
  165.5 31.0 %copy-start = (s32[120]{0:T(128)S(1)}, s32[120]{0:T(128)}, u32[]{:S(2)}) copy-start(s32[120]{0:T(128)} %constant.53) | copy-start | bytes 1444
Sparse Core Ops, SparseCore 0:
  9.8 117.6 all-gather.2
where the time goes:
time: 206 us
  other arithmetic  59.9 us (29%)
  waiting for transfers between devices  38.9 us (19%)
  matrix products  37.8 us (18%)
  blocking collectives  24.6 us (12%)
  local copies, waits for them, and re-layouts  15.8 us (8%)
  starting transfers between devices  15.1 us (7%)
  between operations  13.5 us (7%)
    dot_general x1, other arithmetic, pool_rows(): jnp.einsum('sft,ftd->sfd', counts, tables_one, preferred_element_type=jnp...  57.7 us
    all_to_all x1, blocking collectives, local(): lax.all_to_all(outputs, 'tower', split_axis=0, concat_axis=0, tiled=True)  24.6 us
    dot_general x1, matrix products, pool_rows(): jnp.einsum('sft,ftd->sfd', counts, tables_one, preferred_element_type=jnp...  18.9 us
    all_to_all x1, waiting for transfers between devices, local(): lax.all_to_all(keyed, 'dev', split_axis=1, concat_axis=3, tiled=True)  17.6 us
    all_gather x1, waiting for transfers between devices, local(): every_table = lax.all_gather(tables[0], 'dev', axis=0, tiled=True)  14.5 us
    dot_general x1, matrix products, tower_forward(): high = jnp.dot(low, up[0], preferred_element_type=jnp.float32) + bias[0]  12.7 us
    all_to_all x1, starting transfers between devices, local(): lax.all_to_all(counted, 'dev', split_axis=1, concat_axis=3, tiled=True)  11.6 us
    another operation x1, local copies, waits for them, and re-layouts, local(): rows = pooled_block.reshape(towers * finish_count, -1)  6.45 us
  transfers between devices with their start and end apart: 3, of which 3 were waited for; matrix products, arithmetic and copies ran while one was open for 32% of the time, Pallas kernels for 0%

commit v1 on v0

v1 whole, which is shorter than its diff:
```python
import functools

import jax
import jax.numpy as jnp
import numpy as np
from jax import lax
from jax.experimental import pallas as pl
from jax.experimental.pallas import tpu as pltpu
from jax.sharding import PartitionSpec as P

EMB = 128
OUT = 512
MESH = pl.DeviceIdType.MESH
TILE = 256
PROJ_ROWS = 256


def kernel(
    ids_ref,
    len_ref,
    tab_hbm,
    down_hbm,
    up_hbm,
    bias_ref,
    proj_hbm,
    pbias_ref,
    out_ref,
    keys,
    keys_in,
    cols,
    tab,
    sendbuf,
    base,
    down,
    up,
    proj,
    acc,
    low,
    cross,
    outs,
    gath,
    local_sem,
    k_send,
    k_recv,
    t_send,
    t_recv,
    x_send,
    x_recv,
    o_send,
    o_recv,
):
    t = lax.axis_index("tower")
    v = lax.axis_index("dev")
    zh, x = v // 4, v % 4
    right, left, opposite = (zh + 1) % 4, (zh + 3) % 4, (zh + 2) % 4
    zs = (zh, left, right, opposite)

    def on_z(z):
        return (t, z * 4 + x)

    def on_x(step):
        return (t, zh * 4 + (x + step) % 4)

    barrier = pltpu.get_barrier_semaphore()
    for z in (right, left, opposite):
        pl.semaphore_signal(barrier, inc=1, device_id=on_z(z), device_id_type=MESH)
    for step in (1, 2, 3):
        pl.semaphore_signal(barrier, inc=1, device_id=on_x(step), device_id_type=MESH)
    for mask in range(1, 16):
        pl.semaphore_signal(barrier, inc=1, device_id=(t ^ mask, v), device_id_type=MESH)

    own_tab = pltpu.make_async_copy(tab_hbm, tab.at[0], local_sem.at[0])
    own_tab.start()

    slot = lax.broadcasted_iota(jnp.int32, (4, 128), 0)

    def make_keys(b, carry):
        lanes = pl.ds(pl.multiple_of(b * 128, 128), 128)
        halves = []
        for f in range(2):
            row = ids_ref[f, :, lanes]
            live = slot < len_ref[f : f + 1, lanes]
            code = (128 + (row & 127)) << (row >> 7)
            halves.append(jnp.where(live, code, 0))
        keys[b % 4, b // 4] = jnp.concatenate(halves, axis=0)
        return carry

    lax.fori_loop(0, 64, make_keys, 0, unroll=4)

    pl.semaphore_wait(barrier, 21)

    def key_copy(slot_there, z):
        return pltpu.make_async_remote_copy(
            keys.at[z],
            keys_in.at[slot_there - 1],
            k_send.at[slot_there - 1],
            k_recv.at[slot_there - 1],
            device_id=on_z(z),
            device_id_type=MESH,
        )

    key_copies = {1: key_copy(1, right), 2: key_copy(2, left), 3: key_copy(3, opposite)}

    def tab_copy(src, slot_there, f, z):
        return pltpu.make_async_remote_copy(
            src,
            tab.at[slot_there, f],
            t_send.at[slot_there - 1, f],
            t_recv.at[slot_there - 1, f],
            device_id=on_z(z),
            device_id_type=MESH,
        )

    tab_copies = {
        (1, 0): tab_copy(tab_hbm.at[0], 1, 0, right),
        (1, 1): tab_copy(tab_hbm.at[1], 1, 1, right),
        (2, 0): tab_copy(tab_hbm.at[0], 2, 0, left),
        (2, 1): tab_copy(tab_hbm.at[1], 2, 1, left),
        (3, 0): tab_copy(tab.at[1, 0], 3, 0, right),
        (3, 1): tab_copy(tab.at[2, 1], 3, 1, left),
    }
    key_copies[1].start()
    key_copies[2].start()
    tab_copies[1, 0].start()
    tab_copies[2, 1].start()
    key_copies[3].start()
    tab_copies[1, 1].start()
    tab_copies[2, 0].start()

    weights = [
        pltpu.make_async_copy(down_hbm, down, local_sem.at[1]),
        pltpu.make_async_copy(up_hbm, up, local_sem.at[2]),
        pltpu.make_async_copy(proj_hbm, proj, local_sem.at[3]),
    ]

    def turn(rel):
        def one(b, carry):
            block = keys[zh, b] if rel == 0 else keys_in[rel - 1, b]
            turned = block.astype(jnp.float32).T.astype(jnp.bfloat16)
            rows = pl.ds(pl.multiple_of(b * 32, 32), 32)
            for part in range(4):
                cols[rel, part, rows, :] = turned[32 * part : 32 * part + 32]
            return carry

        lax.fori_loop(0, 16, one, 0, unroll=2)

    row_id = lax.broadcasted_iota(jnp.int32, (1, 1024), 1)
    codes = ((128 + (row_id & 127)) << (row_id >> 7)).astype(jnp.float32).astype(jnp.bfloat16)
    one_b, zero_b = jnp.bfloat16(1), jnp.bfloat16(0)

    def tile_of(rel, f, member, r0):
        rows = cols[rel, member, pl.ds(r0, TILE), 4 * f : 4 * f + 4]
        count = None
        for p in range(4):
            hit = jnp.where(rows[:, p : p + 1] == codes, one_b, zero_b)
            count = hit if count is None else count + hit
        summed = jnp.dot(count, tab[rel, f], preferred_element_type=jnp.float32)
        return summed.astype(jnp.bfloat16)

    def columns_of(rel, f):
        return pl.ds(pl.multiple_of(((zs[rel] * 4 + x) * 2 + f) * EMB, EMB), EMB)

    def x_copy(rel, f, step):
        return pltpu.make_async_remote_copy(
            sendbuf.at[step - 1, rel, f],
            base.at[:, columns_of(rel, f)],
            x_send.at[step - 1, rel, f],
            x_recv.at[step - 1, rel, f],
            device_id=on_x(step),
            device_id_type=MESH,
        )

    def pool(rel, f):
        def to_member(i, carry):
            step = lax.select(i == 0, 2, lax.select(i == 1, 1, 3))
            member = (x + step) % 4
            for piece in range(512 // TILE):
                sendbuf[step - 1, rel, f, pl.ds(piece * TILE, TILE)] = tile_of(
                    rel, f, member, piece * TILE
                )
            x_copy(rel, f, step).start()
            return carry

        lax.fori_loop(0, 3, to_member, 0)
        for piece in range(512 // TILE):
            base[pl.ds(piece * TILE, TILE), columns_of(rel, f)] = tile_of(
                rel, f, x, piece * TILE
            )

    def lower(rel, first):
        for f in range(2):
            for step in (1, 2, 3):
                x_copy(rel, f, step).wait_recv()
        part = pl.ds(pl.multiple_of(zs[rel] * 1024, 1024), 1024)
        term = jnp.dot(base[:, part], down[part, :], preferred_element_type=jnp.float32)
        if first:
            acc[...] = term
        else:
            acc[...] += term

    own_tab.wait()
    turn(0)
    pool(0, 0)
    for copy in weights:
        copy.start()
    pool(0, 1)
    for rel in (1, 2):
        key_copies[rel].wait_recv()
        turn(rel)
    tab_copies[1, 0].wait_recv()
    tab_copies[3, 0].start()
    pool(1, 0)
    tab_copies[2, 1].wait_recv()
    tab_copies[3, 1].start()
    pool(2, 1)
    for copy in weights:
        copy.wait()
    lower(0, True)
    key_copies[3].wait_recv()
    turn(3)
    tab_copies[1, 1].wait_recv()
    pool(1, 1)
    tab_copies[2, 0].wait_recv()
    pool(2, 0)
    tab_copies[3, 0].wait_recv()
    pool(3, 0)
    tab_copies[3, 1].wait_recv()
    pool(3, 1)
    lower(1, False)
    lower(2, False)
    lower(3, False)

    low[...] = acc[...].astype(jnp.bfloat16)
    for n in range(16):
        c = slice(256 * n, 256 * n + 256)
        high = jnp.dot(low[...], up[:, c], preferred_element_type=jnp.float32) + bias_ref[:, c]
        b = base[:, c].astype(jnp.float32)
        cross[:, c] = (b * high + b).astype(jnp.bfloat16)

    per = PROJ_ROWS // 32

    def out_copy(mask):
        return pltpu.make_async_remote_copy(
            outs.at[t ^ mask],
            gath.at[t],
            o_send.at[mask],
            o_recv.at[mask],
            device_id=(t ^ mask, v),
            device_id_type=MESH,
        )

    for chunk in range(512 // PROJ_ROWS):
        group = (t // per) ^ chunk
        r0 = pl.multiple_of(group * PROJ_ROWS, PROJ_ROWS)
        value = jnp.dot(
            cross[pl.ds(r0, PROJ_ROWS), :], proj[...], preferred_element_type=jnp.float32
        )
        value = (value + pbias_ref[...]).astype(jnp.bfloat16)
        outs[pl.ds(group * per, per)] = value.reshape(per, 32, OUT)
        for i in range(per):
            mask = chunk * per + i
            if mask:
                out_copy(mask).start()
    gath[t] = outs[t]
    for mask in range(1, 16):
        out_copy(mask).wait_recv()
    out_ref[...] = gath[...]

    for copy in key_copies.values():
        copy.wait_send()
    for copy in tab_copies.values():
        copy.wait_send()
    for rel in range(4):
        for f in range(2):
            for step in (1, 2, 3):
                x_copy(rel, f, step).wait_send()
    for mask in range(1, 16):
        out_copy(mask).wait_send()


def local(bag_ids, bag_lengths, tables, cross_down, cross_up, cross_bias, proj_weight, proj_bias):
    towers = 16
    bf, i32, f32 = jnp.bfloat16, jnp.int32, jnp.float32
    vmem = pl.BlockSpec(memory_space=pltpu.VMEM)
    hbm = pl.BlockSpec(memory_space=pl.ANY)
    dma = pltpu.SemaphoreType.DMA
    gathered = pl.pallas_call(
        kernel,
        out_shape=jax.ShapeDtypeStruct((16, 32, OUT), bf),
        in_specs=[vmem, vmem, hbm, hbm, hbm, vmem, hbm, vmem],
        out_specs=vmem,
        scratch_shapes=[
            pltpu.VMEM((4, 16, 8, 128), i32),
            pltpu.VMEM((3, 16, 8, 128), i32),
            pltpu.VMEM((4, 4, 512, 8), bf),
            pltpu.VMEM((4, 2, 1024, EMB), bf),
            pltpu.VMEM((3, 4, 2, 512, EMB), bf),
            pltpu.VMEM((512, 4096), bf),
            pltpu.VMEM((4096, 512), bf),
            pltpu.VMEM((512, 4096), bf),
            pltpu.VMEM((4096, 512), bf),
            pltpu.VMEM((512, 512), f32),
            pltpu.VMEM((512, 512), bf),
            pltpu.VMEM((512, 4096), bf),
            pltpu.VMEM((16, 32, OUT), bf),
            pltpu.VMEM((16, 32, OUT), bf),
            dma((4,)),
            dma((3,)),
            dma((3,)),
            dma((3, 2)),
            dma((3, 2)),
            dma((3, 4, 2)),
            dma((3, 4, 2)),
            dma((16,)),
            dma((16,)),
        ],
        compiler_params=pltpu.CompilerParams(
            collective_id=0, has_side_effects=True, vmem_limit_bytes=60 << 20
        ),
    )(
        bag_ids[0].transpose(1, 2, 0),
        bag_lengths[0].transpose(1, 0),
        tables[0],
        cross_down[0, 0],
        cross_up[0, 0],
        cross_bias[0],
        proj_weight[0],
        proj_bias,
    )
    gram = jnp.einsum(
        "isk,jsk->sij", gathered, gathered, preferred_element_type=jnp.float32
    ) / jnp.sqrt(jnp.float32(OUT))
    upper, lower = np.triu_indices(towers, 1)
    return gram[:, upper, lower]


def solution(mesh):
    placed = (
        P("tower", None, "dev", None),
        P("tower", None, "dev"),
        P("tower", "dev", None, None),
        P("tower", None, None, None),
        P("tower", None, None, None),
        P("tower", None, None),
        P("tower", None, None),
        P("tower", None),
    )
    return jax.shard_map(
        local, mesh=mesh, in_specs=placed, out_specs=P(("tower", "dev"), None), check_vma=False
    )
```

time: 206 us -> 90.7 us (0.44)
  Pallas kernels: 0 us -> 85.5 us
  other arithmetic: 59.9 us -> 0 us
  waiting for transfers between devices: 38.9 us -> 0 us
  matrix products: 37.8 us -> 1.87 us
  blocking collectives: 24.6 us -> 0 us
  starting transfers between devices: 15.1 us -> 0 us
  between operations: 13.5 us -> 0.01 us
  local copies, waits for them, and re-layouts: 15.8 us -> 2.45 us
    pallas_call x0 -> x1, Pallas kernels: none -> 85.5 us  [local(): pl.pallas_call(kernel, out_shape=jax.ShapeDtypeStruct((16, 32, OUT), bf),...]
    dot_general x1 -> x0, other arithmetic: 57.7 us -> none  [pool_rows(): jnp.einsum('sft,ftd->sfd', counts, tables_one, preferred_element_type=jnp...]
    dot_general x3 -> x0, matrix products: 37.4 us -> none  [the longest x1 18.9 us: pool_rows(): jnp.einsum('sft,ftd->sfd', counts, tables_one, preferred_element_type=jnp...]
    all_to_all x1 -> x0, blocking collectives: 24.6 us -> none  [local(): lax.all_to_all(outputs, 'tower', split_axis=0, concat_axis=0, tiled=True)]
    all_to_all x2 -> x0, waiting for transfers between devices: 23.7 us -> none  [the longest x1 17.6 us: local(): lax.all_to_all(keyed, 'dev', split_axis=1, concat_axis=3, tiled=True)]
    all_to_all x2 -> x0, starting transfers between devices: 15.1 us -> none  [the longest x1 11.6 us: local(): lax.all_to_all(counted, 'dev', split_axis=1, concat_axis=3, tiled=True)]
    all_gather x1 -> x0, waiting for transfers between devices: 14.5 us -> none  [local(): every_table = lax.all_gather(tables[0], 'dev', axis=0, tiled=True)]
    another operation x5 -> x0, local copies, waits for them, and re-layouts: 9.17 us -> none  [the longest x1 6.45 us: local(): rows = pooled_block.reshape(towers * finish_count, -1)]
  transfers between devices with their start and end apart: 3 -> 0, of which waited for: 3 -> 0; matrix products, arithmetic and copies ran while one was open for 32% -> 0% of each run, Pallas kernels for 0% -> 0%
where the time goes in v1:
time: 90.7 us; the launch traced here: 89.8 us
  Pallas kernels  85.5 us (94%)
  local copies, waits for them, and re-layouts  2.45 us (3%)
  matrix products  1.87 us (2%)
    pallas_call x1, Pallas kernels, local(): pl.pallas_call(kernel, out_shape=jax.ShapeDtypeStruct((16, 32, OUT), bf),...  85.5 us
    gather x2, local copies, waits for them, and re-layouts, local(): return gram[:, upper, lower]  2.28 us
    dot_general x1, matrix products, local(): jnp.einsum('isk,jsk->sij', gathered, gathered, preferred_element_type=jnp...  1.87 us

profile of v1, /device:TPU:1, one launch (start us, length us, event | category | flops | bytes accessed | tf_op | source)
XLA Modules:
  0.0 89.8 jit_solution(11321729369834431363)
XLA Ops:
  0.0 0.0 copy-start
  0.0 85.5 %shard_map.118 = bf16[16,32,512]{2,1,0:T(8,128)(2,1)} custom-call(s32[2,4,8192]{2,1,0:T(4,128)} %bitcast.16, s32[2,8192]{1,0:T(2,128)} %bitcast.18, bf16[2,1024,128]{2,1,0:T(8,128)(2,1)} %bitcast.15, bf16[4096,512]{1,0:T(8,128)(2,1)} %bitcast.12, bf16[512,4096]{1,0:T(8,128)(2,1)} %bitcast.13, f32[1,4096]{1,0:T(1,128)} %bitcast.19, ...), custom_call_target="tpu_custom_call" | custom-call | tf_op jit(solution)/shard_map/pallas_call | solution.py:287
  85.5 1.9 %convolution_multiply_fusion = f32[32,16,16]{2,1,0:T(8,128)S(1)} fusion(bf16[16,32,512]{2,1,0:T(8,128)(2,1)} %shard_map.118), kind=kOutput, calls=%fused_computation.1 | convolution fusion | flops 8396800 | bytes 557056 | tf_op jit(solution)/shard_map/isk,jsk->sij/dot_general | solution.py:330
  87.4 0.2 copy.15
  87.5 0.0 copy-done
  87.5 1.6 %gather_fusion = f32[120,32]{1,0:T(8,128)S(1)} fusion(f32[32,16,16]{0,2,1:T(8,128)S(1)} %copy.15, s32[120]{0:T(128)S(1)} %copy-done), kind=kCustom, calls=%fused_computation | custom fusion | bytes 31680 | tf_op jit(solution)/shard_map/gather | solution.py:334
  89.1 0.7 copy.16
Async XLA Ops:
  0.0 87.5 %copy-start = (s32[120]{0:T(128)S(1)}, s32[120]{0:T(128)}, u32[]{:S(2)}) copy-start(s32[120]{0:T(128)} %constant.45) | copy-start | bytes 1444

commit v2 on v1

v2 whole, which is shorter than its diff:
```python
import functools

import jax
import jax.numpy as jnp
from jax import lax
from jax.experimental import pallas as pl
from jax.experimental.pallas import tpu as pltpu
from jax.sharding import PartitionSpec as P

EMB = 128
OUT = 512
MESH = pl.DeviceIdType.MESH
HALF = 256


def kernel(
    ids_hbm,
    len_hbm,
    tab_hbm,
    down_hbm,
    up_hbm,
    bias_hbm,
    proj_hbm,
    pbias_hbm,
    out_ref,
    ids_ref,
    len_ref,
    bias_ref,
    pbias_ref,
    keys,
    keys_in,
    cols,
    tab,
    sendbuf,
    base,
    down,
    up,
    proj,
    acc,
    low,
    cross,
    outs,
    gath,
    local_sem,
    k_send,
    k_recv,
    t_send,
    t_recv,
    f_send,
    f_recv,
    x_send,
    x_recv,
    o_send,
    o_recv,
):
    t = lax.axis_index("tower")
    v = lax.axis_index("dev")
    zh, x = v // 4, v % 4
    core, place = t % 2, t // 2
    right, left, opposite = (zh + 1) % 4, (zh + 3) % 4, (zh + 2) % 4
    zs = (zh, left, right, opposite)

    def on_z(z):
        return (t, z * 4 + x)

    def on_x(step):
        return (t, zh * 4 + (x + step) % 4)

    def half_of(chunk):
        return (core + chunk) % 2

    def rows_of(chunk):
        return pl.ds(pl.multiple_of(half_of(chunk) * HALF, HALF), HALF)

    barrier = pltpu.get_barrier_semaphore()
    for z in (right, left, opposite):
        pl.semaphore_signal(barrier, inc=1, device_id=on_z(z), device_id_type=MESH)
    for step in (1, 2, 3):
        pl.semaphore_signal(barrier, inc=1, device_id=on_x(step), device_id_type=MESH)
    for mask in range(1, 16):
        pl.semaphore_signal(barrier, inc=1, device_id=(t ^ mask, v), device_id_type=MESH)

    def fetch(k, src, dst):
        return pltpu.make_async_copy(src, dst, local_sem.at[k])

    first = [fetch(0, ids_hbm, ids_ref), fetch(1, len_hbm, len_ref)]
    own_tab = fetch(2, tab_hbm, tab.at[0])
    weights = [
        fetch(3, down_hbm, down),
        fetch(4, up_hbm, up),
        fetch(5, proj_hbm, proj),
        fetch(6, bias_hbm, bias_ref),
        fetch(7, pbias_hbm, pbias_ref),
    ]
    for copy in first:
        copy.start()
    own_tab.start()
    for copy in first:
        copy.wait()

    slot = lax.broadcasted_iota(jnp.int32, (4, 128), 0)

    def make_keys(b, carry):
        z, pair = b % 4, b // 4
        for f in range(2):
            halves = []
            for odd in range(2):
                start = (pair * 2 + odd) * 512 + z * 128
                lanes = pl.ds(pl.multiple_of(start, 128), 128)
                row = ids_ref[f, :, lanes]
                live = slot < len_ref[f : f + 1, lanes]
                code = (128 + (row & 127)) << (row >> 7)
                halves.append(jnp.where(live, code, 0))
            keys[z, f, pair] = jnp.concatenate(halves, axis=0)
        return carry

    lax.fori_loop(0, 32, make_keys, 0, unroll=2)

    def key_copy(there, f):
        z = (None, right, left, opposite)[there]
        return pltpu.make_async_remote_copy(
            keys.at[z, f],
            keys_in.at[there - 1, f],
            k_send.at[there - 1, f],
            k_recv.at[there - 1, f],
            device_id=on_z(z),
            device_id_type=MESH,
        )

    def tab_copy(there, f):
        return pltpu.make_async_remote_copy(
            tab_hbm.at[f],
            tab.at[there, f],
            t_send.at[there - 1, f],
            t_recv.at[there - 1, f],
            device_id=on_z((None, right, left)[there]),
            device_id_type=MESH,
        )

    def forward(there, f):
        rows = pl.ds((there - 1) * 512, 512)
        return pltpu.make_async_remote_copy(
            tab.at[there, f, rows],
            tab.at[3, f, rows],
            f_send.at[there - 1, f],
            f_recv.at[there - 1, f],
            device_id=on_z((None, right, left)[there]),
            device_id_type=MESH,
        )

    def turn(rel, f):
        def one(b, carry):
            block = keys[zh, f, b] if rel == 0 else keys_in[rel - 1, f, b]
            turned = block.astype(jnp.float32).T.astype(jnp.bfloat16)
            rows = pl.ds(pl.multiple_of(b * 32, 32), 32)
            for part in range(4):
                for odd in range(2):
                    cols[rel, f, part, odd, rows, :] = turned[
                        32 * part : 32 * part + 32, 4 * odd : 4 * odd + 4
                    ]
            return carry

        lax.fori_loop(0, 8, one, 0, unroll=2)

    row_id = lax.broadcasted_iota(jnp.int32, (1, 1024), 1)
    codes = ((128 + (row_id & 127)) << (row_id >> 7)).astype(jnp.float32).astype(jnp.bfloat16)
    one_b, zero_b = jnp.bfloat16(1), jnp.bfloat16(0)

    def tile_of(rel, f, member, half):
        rows = cols[rel, f, member, half]
        count = None
        for p in range(4):
            hit = jnp.where(rows[:, p : p + 1] == codes, one_b, zero_b)
            count = hit if count is None else count + hit
        summed = jnp.dot(count, tab[rel, f], preferred_element_type=jnp.float32)
        return summed.astype(jnp.bfloat16)

    def columns_of(rel, f):
        return pl.ds(pl.multiple_of(((zs[rel] * 4 + x) * 2 + f) * EMB, EMB), EMB)

    def x_copy(rel, f, chunk, step):
        return pltpu.make_async_remote_copy(
            sendbuf.at[step - 1, rel, f, chunk],
            base.at[rows_of(chunk), columns_of(rel, f)],
            x_send.at[step - 1, rel, f, chunk],
            x_recv.at[step - 1, rel, f, chunk],
            device_id=on_x(step),
            device_id_type=MESH,
        )

    def pool(rel, f, chunks=(0, 1), send=True):
        def to_member(i, carry):
            place_in, chunk = i % 3, chunks[0] + i // 3
            step = lax.select(place_in == 0, 2, lax.select(place_in == 1, 1, 3))
            sendbuf[step - 1, rel, f, chunk] = tile_of(rel, f, (x + step) % 4, half_of(chunk))
            if send:
                x_copy(rel, f, chunk, step).start()
            return carry

        lax.fori_loop(0, 3 * len(chunks), to_member, 0)

        def to_self(i, carry):
            chunk = chunks[0] + i
            base[rows_of(chunk), columns_of(rel, f)] = tile_of(rel, f, x, half_of(chunk))
            return carry

        lax.fori_loop(0, len(chunks), to_self, 0)

    def part_of(rel):
        return pl.ds(pl.multiple_of(zs[rel] * 1024, 1024), 1024)

    def arrived(rel, chunk):
        for f in range(2):
            for step in (1, 2, 3):
                x_copy(rel, f, chunk, step).wait_recv()

    def lower(rel):
        arrived(rel, 0)
        arrived(rel, 1)
        part = part_of(rel)
        term = jnp.dot(base[:, part], down[part, :], preferred_element_type=jnp.float32)
        if rel == 0:
            acc[...] = term
        else:
            acc[...] += term

    turn(0, 0)
    own_tab.wait()
    pool(0, 0, send=False)
    pl.semaphore_wait(barrier, 21)
    for there in (1, 2):
        key_copy(there, 0).start()
        tab_copy(there, 0).start()
    for chunk in range(2):
        for step in (2, 1, 3):
            x_copy(0, 0, chunk, step).start()
    for there in (1, 2, 3):
        key_copy(there, 1).start()
    key_copy(3, 0).start()
    for there in (1, 2):
        tab_copy(there, 1).start()
    turn(0, 1)
    pool(0, 1)
    for copy in weights:
        copy.start()
    for f in range(2):
        for rel in (1, 2):
            key_copy(rel, f).wait_recv()
            turn(rel, f)
        for rel in (1, 2):
            tab_copy(rel, f).wait_recv()
            forward(rel, f).start()
        for rel in (1, 2):
            pool(rel, f)
        if f == 0:
            for copy in weights:
                copy.wait()
            lower(0)
    for f in range(2):
        key_copy(3, f).wait_recv()
        turn(3, f)
    for f in range(2):
        for there in (1, 2):
            forward(there, f).wait_recv()
        pool(3, f, (0,))
    for f in range(2):
        pool(3, f, (1,))
    lower(1)
    lower(2)

    def out_copy(mask):
        return pltpu.make_async_remote_copy(
            outs.at[t ^ mask],
            gath.at[t],
            o_send.at[mask],
            o_recv.at[mask],
            device_id=(t ^ mask, v),
            device_id_type=MESH,
        )

    for chunk in range(2):
        r = rows_of(chunk)
        arrived(3, chunk)
        part = part_of(3)
        total = acc[r, :] + jnp.dot(
            base[r, part], down[part, :], preferred_element_type=jnp.float32
        )
        low[...] = total.astype(jnp.bfloat16)
        for n in range(16):
            c = slice(256 * n, 256 * n + 256)
            high = jnp.dot(low[...], up[:, c], preferred_element_type=jnp.float32) + bias_ref[:, c]
            b = base[r, c].astype(jnp.float32)
            cross[:, c] = (b * high + b).astype(jnp.bfloat16)
        value = jnp.dot(cross[...], proj[...], preferred_element_type=jnp.float32)
        value = (value + pbias_ref[...]).astype(jnp.bfloat16).reshape(8, 32, OUT)
        for i in range(8):
            outs[2 * i + half_of(chunk)] = value[i]
        for i in range(8):
            mask = 2 * i + chunk
            if mask:
                out_copy(mask).start()
    gath[t] = outs[t]
    for mask in range(1, 16):
        out_copy(mask).wait_recv()

    full = gath[...].reshape(512, OUT)
    gram = lax.dot_general(
        full, full, (((1,), (1,)), ((), ())), preferred_element_type=jnp.float32
    )
    same = (
        lax.broadcasted_iota(jnp.int32, (512, 512), 0) % 32
        == lax.broadcasted_iota(jnp.int32, (512, 512), 1) % 32
    )
    gram = jnp.where(same, gram, 0.0)
    fold = (
        lax.broadcasted_iota(jnp.int32, (512, 128), 0) // 32
        == lax.broadcasted_iota(jnp.int32, (512, 128), 1)
    ).astype(jnp.float32).astype(jnp.bfloat16)
    hi = gram.astype(jnp.bfloat16)
    rest = gram - hi.astype(jnp.float32)
    mid = rest.astype(jnp.bfloat16)
    lo = (rest - mid.astype(jnp.float32)).astype(jnp.bfloat16)
    folded = sum(jnp.dot(p, fold, preferred_element_type=jnp.float32) for p in (lo, mid, hi))
    lane = lax.broadcasted_iota(jnp.int32, (32, 128), 1)
    result = jnp.zeros((32, 128), jnp.float32)
    start = 0
    for i in range(15):
        moved = pltpu.roll(folded[32 * i : 32 * i + 32], (start - i - 1) % 128, 1)
        result = jnp.where((lane >= start) & (lane < start + 15 - i), moved, result)
        start += 15 - i
    out_ref[...] = (result / jnp.sqrt(jnp.float32(OUT)))[:, :120]

    for f in range(2):
        for there in (1, 2, 3):
            key_copy(there, f).wait_send()
        for there in (1, 2):
            tab_copy(there, f).wait_send()
            forward(there, f).wait_send()
    for rel in range(4):
        for f in range(2):
            for chunk in range(2):
                for step in (1, 2, 3):
                    x_copy(rel, f, chunk, step).wait_send()
    for mask in range(1, 16):
        out_copy(mask).wait_send()


def local(bag_ids, bag_lengths, tables, cross_down, cross_up, cross_bias, proj_weight, proj_bias):
    bf, i32, f32 = jnp.bfloat16, jnp.int32, jnp.float32
    hbm = pl.BlockSpec(memory_space=pl.ANY)
    dma = pltpu.SemaphoreType.DMA
    return pl.pallas_call(
        kernel,
        out_shape=jax.ShapeDtypeStruct((32, 120), f32),
        in_specs=[hbm] * 8,
        out_specs=pl.BlockSpec(memory_space=pltpu.VMEM),
        scratch_shapes=[
            pltpu.VMEM((2, 4, 8192), i32),
            pltpu.VMEM((2, 8192), i32),
            pltpu.VMEM((1, 4096), f32),
            pltpu.VMEM((1, OUT), f32),
            pltpu.VMEM((4, 2, 8, 8, 128), i32),
            pltpu.VMEM((3, 2, 8, 8, 128), i32),
            pltpu.VMEM((4, 2, 4, 2, HALF, 4), bf),
            pltpu.VMEM((4, 2, 1024, EMB), bf),
            pltpu.VMEM((3, 4, 2, 2, HALF, EMB), bf),
            pltpu.VMEM((512, 4096), bf),
            pltpu.VMEM((4096, 512), bf),
            pltpu.VMEM((512, 4096), bf),
            pltpu.VMEM((4096, 512), bf),
            pltpu.VMEM((512, 512), f32),
            pltpu.VMEM((HALF, 512), bf),
            pltpu.VMEM((HALF, 4096), bf),
            pltpu.VMEM((16, 32, OUT), bf),
            pltpu.VMEM((16, 32, OUT), bf),
            dma((8,)),
            dma((3, 2)),
            dma((3, 2)),
            dma((2, 2)),
            dma((2, 2)),
            dma((2, 2)),
            dma((2, 2)),
            dma((3, 4, 2, 2)),
            dma((3, 4, 2, 2)),
            dma((16,)),
            dma((16,)),
        ],
        compiler_params=pltpu.CompilerParams(
            collective_id=0, has_side_effects=True, vmem_limit_bytes=60 << 20
        ),
    )(
        bag_ids[0].transpose(1, 2, 0),
        bag_lengths[0].transpose(1, 0),
        tables[0],
        cross_down[0, 0],
        cross_up[0, 0],
        cross_bias[0],
        proj_weight[0],
        proj_bias,
    )


def solution(mesh):
    placed = (
        P("tower", None, "dev", None),
        P("tower", None, "dev"),
        P("tower", "dev", None, None),
        P("tower", None, None, None),
        P("tower", None, None, None),
        P("tower", None, None),
        P("tower", None, None),
        P("tower", None),
    )
    return jax.shard_map(
        local, mesh=mesh, in_specs=placed, out_specs=P(("tower", "dev"), None), check_vma=False
    )
```

time: 90.7 us -> 90.7 us (level)
  Pallas kernels: 85.5 us -> 89.2 us
  matrix products: 1.87 us -> 0 us
  local copies, waits for them, and re-layouts: 2.45 us -> 1.32 us
    pallas_call x1, Pallas kernels: 85.5 us -> 89.2 us  [local(): pl.pallas_call(kernel, out_shape=jax.ShapeDtypeStruct((32, 120), f32), in...]
    gather x2 -> x0, local copies, waits for them, and re-layouts: 2.28 us -> none  [local(): return gram[:, upper, lower]]
    dot_general x1 -> x0, matrix products: 1.87 us -> none  [local(): jnp.einsum('isk,jsk->sij', gathered, gathered, preferred_element_type=jnp...]
    unnamed x2 -> x1, local copies, waits for them, and re-layouts: 0.01 us -> 1.32 us
where the time goes in v2:
time: 90.7 us; the launch traced here: 90.6 us
  Pallas kernels  89.2 us (98%)
  local copies, waits for them, and re-layouts  1.32 us (1%)
    pallas_call x1, Pallas kernels, local(): pl.pallas_call(kernel, out_shape=jax.ShapeDtypeStruct((32, 120), f32), in...  89.2 us

profile of v2, /device:TPU:1, one launch (start us, length us, event | category | flops | bytes accessed | tf_op | source)
XLA Modules:
  0.0 90.6 jit_solution(9493215886399531153)
XLA Ops:
  0.0 89.2 %shard_map.82 = f32[32,120]{1,0:T(8,128)} custom-call(s32[2,4,8192]{2,1,0:T(4,128)} %bitcast.15, s32[2,8192]{1,0:T(2,128)} %bitcast.16, bf16[2,1024,128]{2,1,0:T(8,128)(2,1)} %bitcast.14, bf16[4096,512]{1,0:T(8,128)(2,1)} %bitcast.11, bf16[512,4096]{1,0:T(8,128)(2,1)} %bitcast.12, f32[1,4096]{1,0:T(1,128)} %bitcast.17, bf16[4096,512]{1,0:T(8,128)(2,1)} %bitcast.13, ...), custom_call_target="tpu_custom_call" | custom-call | tf_op jit(solution)/shard_map/pallas_call | solution.py:352
  89.2 1.3 %copy.10 = f32[32,120]{1,0:T(8,128)} copy(f32[32,120]{1,0:T(8,128)} %shard_map.82) | data formatting | bytes 30720

commit v3 on v2

--- a/solution.py
+++ b/solution.py
@@ -29,7 +29,8 @@
     pbias_ref,
     keys,
     keys_in,
-    cols,
+    codes,
+    turned,
     tab,
     sendbuf,
     base,
@@ -48,6 +49,8 @@
     t_recv,
     f_send,
     f_recv,
+    own_sem,
+    pace,
     x_send,
     x_recv,
     o_send,
@@ -100,18 +103,18 @@
 
     slot = lax.broadcasted_iota(jnp.int32, (4, 128), 0)
 
-    def make_keys(b, carry):
-        z, pair = b % 4, b // 4
+    def make_keys(n, carry):
+        z, half, b = n % 4, (n // 4) % 2, n // 8
         for f in range(2):
-            halves = []
-            for odd in range(2):
-                start = (pair * 2 + odd) * 512 + z * 128
+            groups = []
+            for o in range(2):
+                start = (4 * b + 2 * o + half) * 512 + z * 128
                 lanes = pl.ds(pl.multiple_of(start, 128), 128)
                 row = ids_ref[f, :, lanes]
                 live = slot < len_ref[f : f + 1, lanes]
                 code = (128 + (row & 127)) << (row >> 7)
-                halves.append(jnp.where(live, code, 0))
-            keys[z, f, pair] = jnp.concatenate(halves, axis=0)
+                groups.append(jnp.where(live, code, 0))
+            keys[z, f, half, b] = jnp.concatenate(groups, axis=0)
         return carry
 
     lax.fori_loop(0, 32, make_keys, 0, unroll=2)
@@ -148,39 +151,47 @@
             device_id_type=MESH,
         )
 
+    row_id = lax.broadcasted_iota(jnp.int32, (1024, 128), 0)
+    codes[...] = ((128 + (row_id & 127)) << (row_id >> 7)).astype(jnp.float32).astype(jnp.bfloat16)
+    lane_of = lax.broadcasted_iota(jnp.int32, (8, 128), 0) % 4
+
     def turn(rel, f):
-        def one(b, carry):
-            block = keys[zh, f, b] if rel == 0 else keys_in[rel - 1, f, b]
-            turned = block.astype(jnp.float32).T.astype(jnp.bfloat16)
-            rows = pl.ds(pl.multiple_of(b * 32, 32), 32)
-            for part in range(4):
-                for odd in range(2):
-                    cols[rel, f, part, odd, rows, :] = turned[
-                        32 * part : 32 * part + 32, 4 * odd : 4 * odd + 4
-                    ]
-            return carry
-
-        lax.fori_loop(0, 8, one, 0, unroll=2)
-
-    row_id = lax.broadcasted_iota(jnp.int32, (1, 1024), 1)
-    codes = ((128 + (row_id & 127)) << (row_id >> 7)).astype(jnp.float32).astype(jnp.bfloat16)
-    one_b, zero_b = jnp.bfloat16(1), jnp.bfloat16(0)
-
-    def tile_of(rel, f, member, half):
-        rows = cols[rel, f, member, half]
-        count = None
-        for p in range(4):
-            hit = jnp.where(rows[:, p : p + 1] == codes, one_b, zero_b)
-            count = hit if count is None else count + hit
-        summed = jnp.dot(count, tab[rel, f], preferred_element_type=jnp.float32)
-        return summed.astype(jnp.bfloat16)
+        turned[f] = tab[rel, f].astype(jnp.float32).T.astype(jnp.bfloat16)
+
+    def tile(rel, f, chunk, b):
+        half = half_of(chunk)
+        key = keys[zh, f, half, b] if rel == 0 else keys_in[rel - 1, f, half, b]
+        key = key.astype(jnp.float32)
+        weight = jnp.ones((8, 128), jnp.float32)
+        for r in (1, 2, 3):
+            other = jnp.where(lane_of >= r, pltpu.roll(key, r, 0), pltpu.roll(key, r + 4, 0))
+            weight = weight + jnp.where(other == key, 1.0, 0.0)
+        counts = []
+        for o in range(2):
+            count = jnp.zeros((1024, 128), jnp.bfloat16)
+            for p in range(4 * o, 4 * o + 4):
+                k, w = (
+                    jnp.tile(jnp.broadcast_to(a[p : p + 1], (16, 128)).astype(jnp.bfloat16), (64, 1))
+                    for a in (key, weight)
+                )
+                count = jnp.where(k == codes[...], w, count)
+            counts.append(count)
+        pooled = jnp.dot(
+            turned[f], jnp.concatenate(counts, axis=1), preferred_element_type=jnp.float32
+        )
+        for o in range(2):
+            block = pooled[:, 128 * o : 128 * o + 128].T.astype(jnp.bfloat16)
+            rows = pl.ds(pl.multiple_of((2 * b + o) * 32, 32), 32)
+            for member in range(4):
+                step = (member - x + 4) % 4
+                sendbuf[step, rel, f, chunk, rows, :] = block[32 * member : 32 * member + 32]
 
     def columns_of(rel, f):
         return pl.ds(pl.multiple_of(((zs[rel] * 4 + x) * 2 + f) * EMB, EMB), EMB)
 
     def x_copy(rel, f, chunk, step):
         return pltpu.make_async_remote_copy(
-            sendbuf.at[step - 1, rel, f, chunk],
+            sendbuf.at[step, rel, f, chunk],
             base.at[rows_of(chunk), columns_of(rel, f)],
             x_send.at[step - 1, rel, f, chunk],
             x_recv.at[step - 1, rel, f, chunk],
@@ -188,23 +199,36 @@
             device_id_type=MESH,
         )
 
-    def pool(rel, f, chunks=(0, 1), send=True):
-        def to_member(i, carry):
-            place_in, chunk = i % 3, chunks[0] + i // 3
-            step = lax.select(place_in == 0, 2, lax.select(place_in == 1, 1, 3))
-            sendbuf[step - 1, rel, f, chunk] = tile_of(rel, f, (x + step) % 4, half_of(chunk))
-            if send:
-                x_copy(rel, f, chunk, step).start()
+    def own_copy(rel, f, chunk):
+        return pltpu.make_async_copy(
+            sendbuf.at[0, rel, f, chunk],
+            base.at[rows_of(chunk), columns_of(rel, f)],
+            own_sem.at[rel, f, chunk],
+        )
+
+    def fill(rel, f, chunk):
+        def one(b, carry):
+            tile(rel, f, chunk, b)
             return carry
 
-        lax.fori_loop(0, 3 * len(chunks), to_member, 0)
-
-        def to_self(i, carry):
-            chunk = chunks[0] + i
-            base[rows_of(chunk), columns_of(rel, f)] = tile_of(rel, f, x, half_of(chunk))
-            return carry
-
-        lax.fori_loop(0, len(chunks), to_self, 0)
+        lax.fori_loop(0, 4, one, 0)
+
+    def give(rel, f, chunk):
+        for step in (2, 1, 3):
+            x_copy(rel, f, chunk, step).start()
+        own_copy(rel, f, chunk).start()
+
+    def pool(rel, f):
+        turn(rel, f)
+        for chunk in range(2):
+            fill(rel, f, chunk)
+            give(rel, f, chunk)
+
+    def tell(stage):
+        pl.semaphore_signal(pace.at[stage], inc=1, device_id=(t ^ 8, v), device_id_type=MESH)
+
+    def hear(stage):
+        pl.semaphore_wait(pace.at[stage], 1)
 
     def part_of(rel):
         return pl.ds(pl.multiple_of(zs[rel] * 1024, 1024), 1024)
@@ -213,6 +237,7 @@
         for f in range(2):
             for step in (1, 2, 3):
                 x_copy(rel, f, chunk, step).wait_recv()
+            own_copy(rel, f, chunk).wait()
 
     def lower(rel):
         arrived(rel, 0)
@@ -224,49 +249,66 @@
         else:
             acc[...] += term
 
+    own_tab.wait()
     turn(0, 0)
-    own_tab.wait()
-    pool(0, 0, send=False)
+    fill(0, 0, 0)
+    fill(0, 0, 1)
     pl.semaphore_wait(barrier, 21)
     for there in (1, 2):
         key_copy(there, 0).start()
         tab_copy(there, 0).start()
-    for chunk in range(2):
-        for step in (2, 1, 3):
-            x_copy(0, 0, chunk, step).start()
-    for there in (1, 2, 3):
-        key_copy(there, 1).start()
-    key_copy(3, 0).start()
-    for there in (1, 2):
-        tab_copy(there, 1).start()
-    turn(0, 1)
+    give(0, 0, 0)
+    give(0, 0, 1)
     pool(0, 1)
     for copy in weights:
         copy.start()
+    for there in (1, 2):
+        key_copy(there, 1).start()
     for f in range(2):
-        for rel in (1, 2):
-            key_copy(rel, f).wait_recv()
-            turn(rel, f)
-        for rel in (1, 2):
-            tab_copy(rel, f).wait_recv()
-            forward(rel, f).start()
-        for rel in (1, 2):
-            pool(rel, f)
-        if f == 0:
-            for copy in weights:
-                copy.wait()
-            lower(0)
+        key_copy(3, f).start()
+    for there in (1, 2):
+        tab_copy(there, 0).wait_send()
+    tell(0)
+    for rel in (1, 2):
+        key_copy(rel, 0).wait_recv()
+        tab_copy(rel, 0).wait_recv()
+        pool(rel, 0)
+        if rel == 1:
+            hear(0)
+            for there in (1, 2):
+                tab_copy(there, 1).start()
+    for copy in weights:
+        copy.wait()
+    lower(0)
+    for there in (1, 2):
+        tab_copy(there, 1).wait_send()
+    tell(1)
+    for rel in (1, 2):
+        key_copy(rel, 1).wait_recv()
+        tab_copy(rel, 1).wait_recv()
+        pool(rel, 1)
+        if rel == 1:
+            hear(1)
+            for there in (1, 2):
+                forward(there, 0).start()
+    for there in (1, 2):
+        forward(there, 0).wait_send()
+        forward(there, 1).start()
     for f in range(2):
         key_copy(3, f).wait_recv()
-        turn(3, f)
-    for f in range(2):
         for there in (1, 2):
             forward(there, f).wait_recv()
-        pool(3, f, (0,))
-    for f in range(2):
-        pool(3, f, (1,))
+        turn(3, f)
+        fill(3, f, 0)
+        give(3, f, 0)
+        fill(3, f, 1)
     lower(1)
     lower(2)
+    for f in range(2):
+        for step in (1, 2, 3):
+            x_copy(3, f, 0, step).wait_send()
+    for f in range(2):
+        give(3, f, 1)
 
     def out_copy(mask):
         return pltpu.make_async_remote_copy(
@@ -333,14 +375,14 @@
     for f in range(2):
         for there in (1, 2, 3):
             key_copy(there, f).wait_send()
-        for there in (1, 2):
-            tab_copy(there, f).wait_send()
-            forward(there, f).wait_send()
+    for there in (1, 2):
+        forward(there, 1).wait_send()
     for rel in range(4):
         for f in range(2):
             for chunk in range(2):
-                for step in (1, 2, 3):
-                    x_copy(rel, f, chunk, step).wait_send()
+                if (rel, chunk) != (3, 0):
+                    for step in (1, 2, 3):
+                        x_copy(rel, f, chunk, step).wait_send()
     for mask in range(1, 16):
         out_copy(mask).wait_send()
 
@@ -359,11 +401,12 @@
             pltpu.VMEM((2, 8192), i32),
             pltpu.VMEM((1, 4096), f32),
             pltpu.VMEM((1, OUT), f32),
-            pltpu.VMEM((4, 2, 8, 8, 128), i32),
-            pltpu.VMEM((3, 2, 8, 8, 128), i32),
-            pltpu.VMEM((4, 2, 4, 2, HALF, 4), bf),
+            pltpu.VMEM((4, 2, 2, 4, 8, 128), i32),
+            pltpu.VMEM((3, 2, 2, 4, 8, 128), i32),
+            pltpu.VMEM((1024, 128), bf),
+            pltpu.VMEM((2, EMB, 1024), bf),
             pltpu.VMEM((4, 2, 1024, EMB), bf),
-            pltpu.VMEM((3, 4, 2, 2, HALF, EMB), bf),
+            pltpu.VMEM((4, 4, 2, 2, HALF, EMB), bf),
             pltpu.VMEM((512, 4096), bf),
             pltpu.VMEM((4096, 512), bf),
             pltpu.VMEM((512, 4096), bf),
@@ -380,6 +423,8 @@
             dma((2, 2)),
             dma((2, 2)),
             dma((2, 2)),
+            dma((4, 2, 2)),
+            pltpu.SemaphoreType.REGULAR((2,)),
             dma((3, 4, 2, 2)),
             dma((3, 4, 2, 2)),
             dma((16,)),

time: 90.7 us -> 83.2 us (0.917)
  Pallas kernels: 89.2 us -> 81.7 us
    pallas_call x1, Pallas kernels: 89.2 us -> 81.7 us  [local(): pl.pallas_call(kernel, out_shape=jax.ShapeDtypeStruct((32, 120), f32), in...]
where the time goes in v3:
time: 83.2 us; the launch traced here: 83 us
  Pallas kernels  81.7 us (98%)
  local copies, waits for them, and re-layouts  1.32 us (2%)
    pallas_call x1, Pallas kernels, local(): pl.pallas_call(kernel, out_shape=jax.ShapeDtypeStruct((32, 120), f32), in...  81.7 us

profile of v3, /device:TPU:1, one launch (start us, length us, event | category | flops | bytes accessed | tf_op | source)
XLA Modules:
  0.0 83.0 jit_solution(3204812250393017087)
XLA Ops:
  0.0 81.7 %shard_map.82 = f32[32,120]{1,0:T(8,128)} custom-call(s32[2,4,8192]{2,1,0:T(4,128)} %bitcast.15, s32[2,8192]{1,0:T(2,128)} %bitcast.16, bf16[2,1024,128]{2,1,0:T(8,128)(2,1)} %bitcast.14, bf16[4096,512]{1,0:T(8,128)(2,1)} %bitcast.11, bf16[512,4096]{1,0:T(8,128)(2,1)} %bitcast.12, f32[1,4096]{1,0:T(1,128)} %bitcast.17, bf16[4096,512]{1,0:T(8,128)(2,1)} %bitcast.13, ...), custom_call_target="tpu_custom_call" | custom-call | tf_op jit(solution)/shard_map/pallas_call | solution.py:394
  81.7 1.3 %copy.10 = f32[32,120]{1,0:T(8,128)} copy(f32[32,120]{1,0:T(8,128)} %shard_map.82) | data formatting | bytes 30720

commit v4 on v3

--- a/solution.py
+++ b/solution.py
@@ -211,7 +211,7 @@
             tile(rel, f, chunk, b)
             return carry
 
-        lax.fori_loop(0, 4, one, 0)
+        lax.fori_loop(0, 4, one, 0, unroll=2)
 
     def give(rel, f, chunk):
         for step in (2, 1, 3):
@@ -262,53 +262,44 @@
     pool(0, 1)
     for copy in weights:
         copy.start()
-    for there in (1, 2):
-        key_copy(there, 1).start()
-    for f in range(2):
-        key_copy(3, f).start()
-    for there in (1, 2):
-        tab_copy(there, 0).wait_send()
-    tell(0)
-    for rel in (1, 2):
-        key_copy(rel, 0).wait_recv()
-        tab_copy(rel, 0).wait_recv()
-        pool(rel, 0)
-        if rel == 1:
-            hear(0)
-            for there in (1, 2):
-                tab_copy(there, 1).start()
-    for copy in weights:
-        copy.wait()
-    lower(0)
-    for there in (1, 2):
-        tab_copy(there, 1).wait_send()
-    tell(1)
-    for rel in (1, 2):
-        key_copy(rel, 1).wait_recv()
-        tab_copy(rel, 1).wait_recv()
-        pool(rel, 1)
-        if rel == 1:
-            hear(1)
-            for there in (1, 2):
-                forward(there, 0).start()
+
+    def next_tables():
+        hear(0)
+        for there in (1, 2):
+            key_copy(there, 1).start()
+            tab_copy(there, 1).start()
+
+    def next_forwards():
+        hear(1)
+        for f in range(2):
+            key_copy(3, f).start()
+        for there in (1, 2):
+            forward(there, 0).start()
+
+    for f, advance in ((0, next_tables), (1, next_forwards)):
+        for there in (1, 2):
+            tab_copy(there, f).wait_send()
+        tell(f)
+        advance()
+        for rel in (1, 2):
+            key_copy(rel, f).wait_recv()
+            tab_copy(rel, f).wait_recv()
+            pool(rel, f)
+        if f == 0:
+            for copy in weights:
+                copy.wait()
+            lower(0)
     for there in (1, 2):
         forward(there, 0).wait_send()
         forward(there, 1).start()
     for f in range(2):
+        if f == 1:
+            lower(1)
+            lower(2)
         key_copy(3, f).wait_recv()
         for there in (1, 2):
             forward(there, f).wait_recv()
-        turn(3, f)
-        fill(3, f, 0)
-        give(3, f, 0)
-        fill(3, f, 1)
-    lower(1)
-    lower(2)
-    for f in range(2):
-        for step in (1, 2, 3):
-            x_copy(3, f, 0, step).wait_send()
-    for f in range(2):
-        give(3, f, 1)
+        pool(3, f)
 
     def out_copy(mask):
         return pltpu.make_async_remote_copy(
@@ -361,8 +352,7 @@
     hi = gram.astype(jnp.bfloat16)
     rest = gram - hi.astype(jnp.float32)
     mid = rest.astype(jnp.bfloat16)
-    lo = (rest - mid.astype(jnp.float32)).astype(jnp.bfloat16)
-    folded = sum(jnp.dot(p, fold, preferred_element_type=jnp.float32) for p in (lo, mid, hi))
+    folded = sum(jnp.dot(p, fold, preferred_element_type=jnp.float32) for p in (mid, hi))
     lane = lax.broadcasted_iota(jnp.int32, (32, 128), 1)
     result = jnp.zeros((32, 128), jnp.float32)
     start = 0
@@ -380,9 +370,8 @@
     for rel in range(4):
         for f in range(2):
             for chunk in range(2):
-                if (rel, chunk) != (3, 0):
-                    for step in (1, 2, 3):
-                        x_copy(rel, f, chunk, step).wait_send()
+                for step in (1, 2, 3):
+                    x_copy(rel, f, chunk, step).wait_send()
     for mask in range(1, 16):
         out_copy(mask).wait_send()
 

time: 83.2 us -> 79.8 us (0.959)
  Pallas kernels: 81.7 us -> 78.3 us
    pallas_call x1, Pallas kernels: 81.7 us -> 78.3 us  [local(): pl.pallas_call(kernel, out_shape=jax.ShapeDtypeStruct((32, 120), f32), in...]
where the time goes in v4:
time: 79.8 us; the launch traced here: 79.7 us
  Pallas kernels  78.3 us (98%)
  local copies, waits for them, and re-layouts  1.32 us (2%)
    pallas_call x1, Pallas kernels, local(): pl.pallas_call(kernel, out_shape=jax.ShapeDtypeStruct((32, 120), f32), in...  78.3 us

profile of v4, /device:TPU:1, one launch (start us, length us, event | category | flops | bytes accessed | tf_op | source)
XLA Modules:
  0.0 79.7 jit_solution(15747863472445931002)
XLA Ops:
  0.0 78.3 %shard_map.82 = f32[32,120]{1,0:T(8,128)} custom-call(s32[2,4,8192]{2,1,0:T(4,128)} %bitcast.15, s32[2,8192]{1,0:T(2,128)} %bitcast.16, bf16[2,1024,128]{2,1,0:T(8,128)(2,1)} %bitcast.14, bf16[4096,512]{1,0:T(8,128)(2,1)} %bitcast.11, bf16[512,4096]{1,0:T(8,128)(2,1)} %bitcast.12, f32[1,4096]{1,0:T(1,128)} %bitcast.17, bf16[4096,512]{1,0:T(8,128)(2,1)} %bitcast.13, ...), custom_call_target="tpu_custom_call" | custom-call | tf_op jit(solution)/shard_map/pallas_call | solution.py:383
  78.3 1.3 %copy.10 = f32[32,120]{1,0:T(8,128)} copy(f32[32,120]{1,0:T(8,128)} %shard_map.82) | data formatting | bytes 30720

commit v5 on v4

--- a/solution.py
+++ b/solution.py
@@ -252,12 +252,12 @@
     own_tab.wait()
     turn(0, 0)
     fill(0, 0, 0)
-    fill(0, 0, 1)
     pl.semaphore_wait(barrier, 21)
     for there in (1, 2):
         key_copy(there, 0).start()
         tab_copy(there, 0).start()
     give(0, 0, 0)
+    fill(0, 0, 1)
     give(0, 0, 1)
     pool(0, 1)
     for copy in weights:
@@ -268,11 +268,10 @@
         for there in (1, 2):
             key_copy(there, 1).start()
             tab_copy(there, 1).start()
+            key_copy(3, there - 1).start()
 
     def next_forwards():
         hear(1)
-        for f in range(2):
-            key_copy(3, f).start()
         for there in (1, 2):
             forward(there, 0).start()
 
@@ -299,7 +298,14 @@
         key_copy(3, f).wait_recv()
         for there in (1, 2):
             forward(there, f).wait_recv()
-        pool(3, f)
+        turn(3, f)
+        fill(3, f, 0)
+        give(3, f, 0)
+        fill(3, f, 1)
+        if f == 1:
+            for step in (1, 2, 3):
+                x_copy(3, 1, 0, step).wait_send()
+        give(3, f, 1)
 
     def out_copy(mask):
         return pltpu.make_async_remote_copy(
@@ -328,7 +334,7 @@
         value = (value + pbias_ref[...]).astype(jnp.bfloat16).reshape(8, 32, OUT)
         for i in range(8):
             outs[2 * i + half_of(chunk)] = value[i]
-        for i in range(8):
+        for i in reversed(range(8)):
             mask = 2 * i + chunk
             if mask:
                 out_copy(mask).start()
@@ -370,8 +376,9 @@
     for rel in range(4):
         for f in range(2):
             for chunk in range(2):
-                for step in (1, 2, 3):
-                    x_copy(rel, f, chunk, step).wait_send()
+                if (rel, f, chunk) != (3, 1, 0):
+                    for step in (1, 2, 3):
+                        x_copy(rel, f, chunk, step).wait_send()
     for mask in range(1, 16):
         out_copy(mask).wait_send()
 

time: 79.8 us -> 78.1 us (0.979)
  Pallas kernels: 78.3 us -> 76.6 us
    pallas_call x1, Pallas kernels: 78.3 us -> 76.6 us  [local(): pl.pallas_call(kernel, out_shape=jax.ShapeDtypeStruct((32, 120), f32), in...]
where the time goes in v5:
time: 78.1 us; the launch traced here: 77.9 us
  Pallas kernels  76.6 us (98%)
  local copies, waits for them, and re-layouts  1.32 us (2%)
    pallas_call x1, Pallas kernels, local(): pl.pallas_call(kernel, out_shape=jax.ShapeDtypeStruct((32, 120), f32), in...  76.6 us

profile of v5, /device:TPU:1, one launch (start us, length us, event | category | flops | bytes accessed | tf_op | source)
XLA Modules:
  0.0 77.9 jit_solution(8241616123890217127)
XLA Ops:
  0.0 76.6 %shard_map.82 = f32[32,120]{1,0:T(8,128)} custom-call(s32[2,4,8192]{2,1,0:T(4,128)} %bitcast.15, s32[2,8192]{1,0:T(2,128)} %bitcast.16, bf16[2,1024,128]{2,1,0:T(8,128)(2,1)} %bitcast.14, bf16[4096,512]{1,0:T(8,128)(2,1)} %bitcast.11, bf16[512,4096]{1,0:T(8,128)(2,1)} %bitcast.12, f32[1,4096]{1,0:T(1,128)} %bitcast.17, bf16[4096,512]{1,0:T(8,128)(2,1)} %bitcast.13, ...), custom_call_target="tpu_custom_call" | custom-call | tf_op jit(solution)/shard_map/pallas_call | solution.py:390
  76.6 1.3 %copy.10 = f32[32,120]{1,0:T(8,128)} copy(f32[32,120]{1,0:T(8,128)} %shard_map.82) | data formatting | bytes 30720

commit v6 on v5

--- a/solution.py
+++ b/solution.py
@@ -271,14 +271,14 @@
             key_copy(3, there - 1).start()
 
     def next_forwards():
-        hear(1)
         for there in (1, 2):
             forward(there, 0).start()
 
     for f, advance in ((0, next_tables), (1, next_forwards)):
         for there in (1, 2):
             tab_copy(there, f).wait_send()
-        tell(f)
+        if f == 0:
+            tell(f)
         advance()
         for rel in (1, 2):
             key_copy(rel, f).wait_recv()
@@ -292,9 +292,6 @@
         forward(there, 0).wait_send()
         forward(there, 1).start()
     for f in range(2):
-        if f == 1:
-            lower(1)
-            lower(2)
         key_copy(3, f).wait_recv()
         for there in (1, 2):
             forward(there, f).wait_recv()
@@ -303,6 +300,8 @@
         give(3, f, 0)
         fill(3, f, 1)
         if f == 1:
+            lower(1)
+            lower(2)
             for step in (1, 2, 3):
                 x_copy(3, 1, 0, step).wait_send()
         give(3, f, 1)
@@ -420,7 +419,7 @@
             dma((2, 2)),
             dma((2, 2)),
             dma((4, 2, 2)),
-            pltpu.SemaphoreType.REGULAR((2,)),
+            pltpu.SemaphoreType.REGULAR((1,)),
             dma((3, 4, 2, 2)),
             dma((3, 4, 2, 2)),
             dma((16,)),

time: 78.1 us -> 78 us (level)
  no operation moved by 1% of the time
where the time goes in v6:
time: 78 us; the launch traced here: 77.8 us
  Pallas kernels  76.5 us (98%)
  local copies, waits for them, and re-layouts  1.32 us (2%)
    pallas_call x1, Pallas kernels, local(): pl.pallas_call(kernel, out_shape=jax.ShapeDtypeStruct((32, 120), f32), in...  76.5 us

profile of v6, /device:TPU:1, one launch (start us, length us, event | category | flops | bytes accessed | tf_op | source)
XLA Modules:
  0.0 77.8 jit_solution(2926294492369838636)
XLA Ops:
  0.0 76.5 %shard_map.82 = f32[32,120]{1,0:T(8,128)} custom-call(s32[2,4,8192]{2,1,0:T(4,128)} %bitcast.15, s32[2,8192]{1,0:T(2,128)} %bitcast.16, bf16[2,1024,128]{2,1,0:T(8,128)(2,1)} %bitcast.14, bf16[4096,512]{1,0:T(8,128)(2,1)} %bitcast.11, bf16[512,4096]{1,0:T(8,128)(2,1)} %bitcast.12, f32[1,4096]{1,0:T(1,128)} %bitcast.17, bf16[4096,512]{1,0:T(8,128)(2,1)} %bitcast.13, ...), custom_call_target="tpu_custom_call" | custom-call | tf_op jit(solution)/shard_map/pallas_call | solution.py:389
  76.5 1.3 %copy.10 = f32[32,120]{1,0:T(8,128)} copy(f32[32,120]{1,0:T(8,128)} %shard_map.82) | data formatting | bytes 30720
